TPU v7x, 32 devices: a whole 2x2x4 slice. The times are simulated.
32 devices in a mesh: dp: 8 (over y, x, core), mp: 4 (over z).
Axes of the slice: x: 2, y: 2, z: 4, core: 2. Of those that a mesh axis runs over, the one named last changes fastest.
Arguments:
- queries: bfloat16 [2048, 2048], P('dp', 'mp'), may hold values from -24 to 24
- context_grad: bfloat16 [2048, 2048], P('dp', 'mp'), may hold values from -6 to 6
- encoder_rows: bfloat16 [7168, 4096], P('dp'), may hold values from -60 to 60
- key_weight: bfloat16 [4096, 2048], P('dp', 'mp'), may hold values from -1 to 1
- value_weight: bfloat16 [4096, 2048], P('dp', 'mp'), may hold values from -0.09375 to 0.09375
- document_lengths: int32 [8, 4], P('dp'), may hold values from 1 to 128, 256 in all within a row
- block_bin: int32 [56], P('dp'), may hold values from 0 to 7, as said below
- block_document: int32 [56], P('dp'), may hold values from 0 to 3
Outputs:
- context: bfloat16 [2048, 2048], P('dp', 'mp')
- query_grad: bfloat16 [2048, 2048], P('dp', 'mp')
- encoder_grad: bfloat16 [7168, 4096], P('dp', 'mp')
- key_weight_grad: bfloat16 [4096, 2048], P('dp', 'mp')
- value_weight_grad: bfloat16 [4096, 2048], P('dp', 'mp')
Inputs may be any that keep to these rules, and one draw needn't show every extreme that they name: `block_bin`: each index of dp holds 7 encoder blocks and sends them to 7 different bins; one bin receives a block from every index of dp.
All inputs are finite; a program needn't handle non-finite values.
Results may differ from a plain program's by a relative error of at most 0.03.
The roundings to bfloat16 on the way count: a program that leaves them out, or rounds other values in their place, can miss the bound.
Values may be sent and summed in bfloat16 or wider, within the bound.
A program may use at most 128 MiB of HBM per device.

v0:
```python
import jax
import jax.numpy as jnp
from jax import lax
from jax.sharding import PartitionSpec as P

HD = 256
BLK = 128
masked_value = -1e30


def attend_weights(scores, live_mask):
    present = jnp.any(live_mask, axis=1)[None, :, None]
    blocked = jnp.where(live_mask[None], scores, masked_value)
    highest = jnp.max(blocked, axis=2, keepdims=True)
    highest = jnp.where(present, highest, 0.0)
    raised = jnp.exp(jnp.where(live_mask[None], scores - highest, masked_value))
    totals = jnp.maximum(jnp.sum(raised, axis=2, keepdims=True), 1.0)
    return raised / totals


def token_documents(lengths, token_count):
    doc_ends = jnp.cumsum(lengths)
    positions = jnp.arange(token_count, dtype=jnp.int32)
    return jnp.sum((doc_ends[None, :] <= positions[:, None]).astype(jnp.int32), axis=1)


def per_device(
    queries,
    context_grad,
    encoder_rows,
    key_weight,
    value_weight,
    document_lengths,
    block_bin,
    block_document,
):
    bin_count = lax.axis_size("dp")
    full_key, full_value = (
        lax.all_gather(key_weight, "dp", axis=0, tiled=True),
        lax.all_gather(value_weight, "dp", axis=0, tiled=True),
    )
    head_width = full_key.shape[1]
    head_count = head_width // HD
    block_rows = BLK
    blocks_here = block_bin.shape[0]
    both_weights = jnp.concatenate([full_key, full_value], axis=1)
    projected = jnp.dot(encoder_rows, both_weights, preferred_element_type=jnp.float32).astype(
        jnp.bfloat16
    )
    route_table = (block_bin[:, None] == jnp.arange(bin_count, dtype=jnp.int32)[None, :]).astype(
        jnp.bfloat16
    )
    flat_blocks = projected.reshape(blocks_here, block_rows * 2 * head_width)
    outbound = lax.dot_general(
        route_table, flat_blocks, (((0,), (0,)), ((), ())), preferred_element_type=jnp.float32
    )
    outbound = outbound.astype(jnp.bfloat16).reshape(bin_count, block_rows, 2 * head_width)
    slot_docs = (
        lax.dot_general(
            route_table.astype(jnp.float32),
            (block_document + 1).astype(jnp.float32),
            (((0,), (0,)), ((), ())),
        )
        - 1.0
    )
    tag_rows = jnp.broadcast_to(slot_docs[:, None], (bin_count, block_rows)).astype(jnp.bfloat16)
    arrived, arrived_tags = (
        lax.all_to_all(outbound, "dp", split_axis=0, concat_axis=0, tiled=True),
        lax.all_to_all(tag_rows, "dp", split_axis=0, concat_axis=0, tiled=True),
    )
    key_slots = arrived[:, :, :head_width].reshape(bin_count * block_rows, head_count, HD)
    value_slots = arrived[:, :, head_width:].reshape(bin_count * block_rows, head_count, HD)
    token_count = queries.shape[0]
    token_docs = token_documents(document_lengths[0], token_count).astype(jnp.float32)
    live_mask = arrived_tags.reshape(-1).astype(jnp.float32)[None, :] == token_docs[:, None]
    query_heads = queries.reshape(token_count, head_count, HD)
    grad_heads = context_grad.reshape(token_count, head_count, HD)
    scaling = HD ** (-0.5)
    scores = (
        jnp.einsum("thd,shd->hts", query_heads, key_slots, preferred_element_type=jnp.float32)
        * scaling
    )
    attention = attend_weights(scores, live_mask)
    rounded = attention.astype(jnp.bfloat16)
    context = jnp.einsum(
        "hts,shd->thd", rounded, value_slots, preferred_element_type=jnp.float32
    ).astype(jnp.bfloat16)
    grad_raw = jnp.einsum(
        "thd,shd->hts", grad_heads, value_slots, preferred_element_type=jnp.float32
    )
    deltas = jnp.sum(attention * grad_raw, axis=2, keepdims=True)
    score_grad = (attention * (grad_raw - deltas) * scaling).astype(jnp.bfloat16)
    query_grad = jnp.einsum(
        "hts,shd->thd", score_grad, key_slots, preferred_element_type=jnp.float32
    ).astype(jnp.bfloat16)
    key_grad = jnp.einsum(
        "hts,thd->shd", score_grad, query_heads, preferred_element_type=jnp.float32
    ).astype(jnp.bfloat16)
    value_grad = jnp.einsum(
        "hts,thd->shd", rounded, grad_heads, preferred_element_type=jnp.float32
    ).astype(jnp.bfloat16)
    slot_grads = jnp.concatenate(
        [
            key_grad.reshape(bin_count, block_rows, head_width),
            value_grad.reshape(bin_count, block_rows, head_width),
        ],
        axis=2,
    )
    returned = lax.all_to_all(slot_grads, "dp", split_axis=0, concat_axis=0, tiled=True)
    own_grads = jnp.dot(
        route_table,
        returned.reshape(bin_count, block_rows * 2 * head_width),
        preferred_element_type=jnp.float32,
    )
    own_grads = own_grads.astype(jnp.bfloat16).reshape(encoder_rows.shape[0], 2 * head_width)
    weight_terms = lax.dot_general(
        encoder_rows, own_grads, (((0,), (0,)), ((), ())), preferred_element_type=jnp.float32
    )
    weight_sums = lax.psum_scatter(
        weight_terms.astype(jnp.bfloat16), "dp", scatter_dimension=0, tiled=True
    ).astype(jnp.float32)
    key_weight_grad = weight_sums[:, :head_width].astype(jnp.bfloat16)
    value_weight_grad = weight_sums[:, head_width:].astype(jnp.bfloat16)
    row_terms = lax.dot_general(
        own_grads, both_weights, (((1,), (1,)), ((), ())), preferred_element_type=jnp.float32
    )
    encoder_grad = lax.psum_scatter(
        row_terms.astype(jnp.bfloat16), "mp", scatter_dimension=1, tiled=True
    )
    return (
        context.reshape(token_count, head_width),
        query_grad.reshape(token_count, head_width),
        encoder_grad,
        key_weight_grad,
        value_weight_grad,
    )


def solution(mesh):
    in_specs = (
        P("dp", "mp"),
        P("dp", "mp"),
        P("dp", None),
        P("dp", "mp"),
        P("dp", "mp"),
        P("dp", None),
        P("dp"),
        P("dp"),
    )
    out_specs = (P("dp", "mp"), P("dp", "mp"), P("dp", "mp"), P("dp", "mp"), P("dp", "mp"))
    return jax.shard_map(
        per_device, mesh=mesh, in_specs=in_specs, out_specs=out_specs, check_vma=False
    )
```

profile of v0, /device:TPU:0, one launch (start us, length us, event | category | flops | bytes accessed | tf_op | source)
XLA Modules:
  0.0 427.2 jit_solution(468431480410873868)
XLA Ops:
  10.2 5.2 %all-to-all-start.1 = ((bf16[8,1,128]{2,1,0:T(2,128)(2,1)}), bf16[8,1,128]{2,1,0:T(2,128)(2,1)S(1)}, u32[]{:S(2)}, u32[]{:S(2)}) async-start(bf16[8,1,128]{2,1,0:T(2,128)(2,1)} %broadcast_in_dim.30), calls=%async_computation.1 | async-start | bytes 8192 | tf_op jit(solution)/shard_map/all_to_all | solution.py:69
  15.4 33.8 %all-gather.3.cloned.1.call-done = bf16[4096,512]{1,0:T(8,128)(2,1)} async-done(((bf16[512,512]{1,0:T(8,128)(2,1)}), bf16[4096,512]{1,0:T(8,128)(2,1)}) %all-gather.3.cloned.1.call-update) | async-done | bytes 4194320 | tf_op jit(solution)/shard_map/all_gather | solution.py:39
  49.2 4.5 %constant_dynamic-update-slice_fusion.1 = bf16[4096,1024]{1,0:T(8,128)(2,1)} fusion(bf16[4096,512]{1,0:T(8,128)(2,1)} %all-gather.3.cloned.1.call-done), kind=kLoop, calls=%fused_computation.43 | loop fusion | bytes 8388608
  53.7 34.0 %all-gather.5.cloned.1.call-done = bf16[4096,512]{1,0:T(8,128)(2,1)} async-done(((bf16[512,512]{1,0:T(8,128)(2,1)}), bf16[4096,512]{1,0:T(8,128)(2,1)}) %all-gather.5.cloned.1.call-update) | async-done | bytes 4194320 | tf_op jit(solution)/shard_map/all_gather | solution.py:40
  87.7 4.5 %constant_dynamic-update-slice_fusion = bf16[4096,1024]{1,0:T(8,128)(2,1)} fusion(bf16[4096,1024]{1,0:T(8,128)(2,1)} %constant_dynamic-update-slice_fusion.1, bf16[4096,512]{1,0:T(8,128)(2,1)} %all-gather.5.cloned.1.call-done), kind=kLoop, calls=%fused_computation.42 | loop fusion | bytes 8388608 | tf_op jit(solution)/shard_map/concatenate | solution.py:46
  92.2 13.4 %convert_bitcast_fusion.1 = bf16[896,1024]{0,1:T(8,128)(2,1)S(1)} fusion(bf16[4096,1024]{1,0:T(8,128)(2,1)} %constant_dynamic-update-slice_fusion, bf16[896,4096]{1,0:T(8,128)(2,1)} %param.10), kind=kOutput, calls=%fused_computation.16 | convolution fusion | flops 7517110272 | bytes 17563648 | tf_op jit(solution)/shard_map/dot_general | solution.py:47
  105.6 2.4 copy.79
  108.0 3.8 reshape.137
  111.8 2.2 convolution_convert_fusion.1
  114.0 4.1 copy.80
  118.2 3.7 all-to-all-start
  122.7 25.8 %all-to-all-done = bf16[8,128,1024]{1,2,0:T(8,128)(2,1)S(1)} async-done(((bf16[8,128,1024]{1,2,0:T(8,128)(2,1)}), bf16[8,128,1024]{1,2,0:T(8,128)(2,1)S(1)}, u32[]{:S(2)}, u32[]{:S(2)}) %all-to-all-start) | async-done | bytes 2097184 | tf_op jit(solution)/shard_map/all_to_all | solution.py:68
  154.9 1.9 fusion.17
  158.4 6.1 %fusion.9 = bf16[1024,2,256]{2,0,1:T(8,128)(2,1)} fusion(f32[2,1024,256]{2,1,0:T(8,128)} %fusion.17, bf16[32,2,8,256]{3,2,1,0:T(8,128)(2,1)} %bitcast.136, f32[2,1024,256]{2,1,0:T(8,128)} %copy-done.1, f32[2,256]{1,0:T(2,128)S(1)} %broadcast_maximum_fusion, f32[2,256]{1,0:T(2,128)S(1)} %broadcast_select_fusion, pred[256,1024]{0,1:T(8,128)(4,1)S(1)} %get-tuple-element.35), kind=kOutput, calls=%fused_computation.21 | convolution fusion | flops 275777024 | bytes 5771264 | tf_op jit(solution)/shard_map/hts,thd->shd/dot_general | solution.py:96
  166.7 29.0 %all_to_all.16 = bf16[8,128,1024]{1,2,0:T(8,128)(2,1)S(1)} all-to-all(bf16[8,128,1024]{1,2,0:T(8,128)(2,1)S(1)} %copy.93), channel_id=1, replica_groups=mesh['dp'=8,'mp'=4] {'dp'}, dimensions={0} | all-to-all | bytes 4194304 | tf_op jit(solution)/shard_map/all_to_all | solution.py:109
  195.7 2.6 copy.94
  198.4 2.7 copy.107
  201.9 4.0 reshape.150
  205.8 13.8 %convert_bitcast_fusion = bf16[4096,1024]{0,1:T(8,128)(2,1)} fusion(bf16[896,1024]{1,0:T(8,128)(2,1)} %reshape.150, bf16[896,4096]{1,0:T(8,128)(2,1)} %param.10), kind=kOutput, calls=%fused_computation.3 | convolution fusion | flops 7520387072 | bytes 17563648 | tf_op jit(solution)/shard_map/dot_general | solution.py:116
  221.1 13.4 %convolution_convert_fusion.2 = bf16[896,4096]{1,0:T(8,128)(2,1)} fusion(bf16[896,1024]{1,0:T(8,128)(2,1)S(1)} %copy-done.3, bf16[4096,1024]{1,0:T(8,128)(2,1)} %constant_dynamic-update-slice_fusion), kind=kOutput, calls=%fused_computation.4 | convolution fusion | flops 7519862784 | bytes 17563648 | tf_op jit(solution)/shard_map/dot_general | solution.py:124
  237.7 1.8 copy.95
  239.5 4.2 convolution_convert_fusion.5
  244.5 45.7 %reduce-scatter.5.cloned.1.call-done = bf16[512,1024]{0,1:T(8,128)(2,1)} async-done(((bf16[4096,1024]{0,1:T(8,128)(2,1)}), bf16[512,1024]{0,1:T(8,128)(2,1)}) %reduce-scatter.5.cloned.1.call-update) | async-done | bytes 1048592 | tf_op jit(solution)/shard_map/reduce_scatter | solution.py:119
  293.5 127.3 %reduce-scatter.3.cloned.1.call-done = bf16[896,1024]{1,0:T(8,128)(2,1)} async-done(((bf16[896,4096]{1,0:T(8,128)(2,1)}), bf16[896,1024]{1,0:T(8,128)(2,1)}) %reduce-scatter.3.cloned.1.call-update) | async-done | bytes 1835024 | tf_op jit(solution)/shard_map/reduce_scatter | solution.py:127
  (54 shorter events, 23.3 us)
Async XLA Ops:
  7.2 42.0 %all-gather.3.cloned.1.call-start = ((), (), s32[]{:S(2)}) async-start(), calls=%async_computation.5 | async-start | bytes 4718592 | tf_op jit(solution)/shard_map/all_gather | solution.py:39
  7.9 79.8 %all-gather.5.cloned.1.call-start = ((), (), s32[]{:S(2)}) async-start(), calls=%async_computation.6 | async-start | bytes 4718592 | tf_op jit(solution)/shard_map/all_gather | solution.py:40
  10.2 108.0 %all-to-all-start.1 = ((bf16[8,1,128]{2,1,0:T(2,128)(2,1)}), bf16[8,1,128]{2,1,0:T(2,128)(2,1)S(1)}, u32[]{:S(2)}, u32[]{:S(2)}) async-start(bf16[8,1,128]{2,1,0:T(2,128)(2,1)} %broadcast_in_dim.30), calls=%async_computation.1 | async-start | bytes 8192 | tf_op jit(solution)/shard_map/all_to_all | solution.py:69
  108.0 3.8 copy-start.6
  118.2 4.0 copy-start.7
  118.2 30.3 %all-to-all-start = ((bf16[8,128,1024]{1,2,0:T(8,128)(2,1)}), bf16[8,128,1024]{1,2,0:T(8,128)(2,1)S(1)}, u32[]{:S(2)}, u32[]{:S(2)}) async-start(bf16[8,128,1024]{1,2,0:T(8,128)(2,1)} %copy.80), calls=%async_computation | async-start | bytes 4194304 | tf_op jit(solution)/shard_map/all_to_all | solution.py:68
  121.9 168.3 %reduce-scatter.5.cloned.1.call-start = ((), (), s32[]{:S(2)}) async-start(), calls=%async_computation.8 | async-start | bytes 9437184 | tf_op jit(solution)/shard_map/reduce_scatter | solution.py:119
  149.6 1.2 copy-start
  152.0 2.3 copy-start.4
  153.8 3.1 copy-start.1
  153.8 1.1 copy-start.5
  219.6 1.5 copy-start.3
  219.6 201.1 %reduce-scatter.3.cloned.1.call-start = ((), (), s32[]{:S(2)}) async-start(), calls=%async_computation.7 | async-start | bytes 9175040 | tf_op jit(solution)/shard_map/reduce_scatter | solution.py:127
  234.5 1.7 copy-start.2
Sparse Core Ops, SparseCore 0:
  9.9 39.2 all-gather.2
  51.1 36.5 all-gather.4
  219.7 70.3 reduce-scatter.4
  292.9 127.7 reduce-scatter.2
where the time goes:
time: 428 us; the launch traced here: 427 us
  waiting for transfers between devices  268 us (63%)
  matrix products  60.6 us (14%)
  local copies, waits for them, and re-layouts  44.9 us (10%)
  blocking collectives  29 us (7%)
  between operations  14 us (3%)
  starting transfers between devices  9.53 us (2%)
    reduce_scatter x1, waiting for transfers between devices, per_device(): lax.psum_scatter(row_terms.astype(jnp.bfloat16), 'mp', scatter_dimension=...  127 us
    reduce_scatter x1, waiting for transfers between devices, per_device(): lax.psum_scatter(weight_terms.astype(jnp.bfloat16), 'dp', scatter_dimensi...  45.7 us
    all_gather x1, waiting for transfers between devices, per_device(): lax.all_gather(value_weight, 'dp', axis=0, tiled=True)  34 us
    all_gather x1, waiting for transfers between devices, per_device(): lax.all_gather(key_weight, 'dp', axis=0, tiled=True)  33.8 us
    all_to_all x1, blocking collectives, per_device(): lax.all_to_all(slot_grads, 'dp', split_axis=0, concat_axis=0, tiled=True)  29 us
    all_to_all x1, waiting for transfers between devices, per_device(): lax.all_to_all(outbound, 'dp', split_axis=0, concat_axis=0, tiled=True)  25.8 us
    unnamed x24, local copies, waits for them, and re-layouts  15.9 us
    dot_general x1, matrix products, per_device(): lax.dot_general(encoder_rows, own_grads, (((0,), (0,)), ((), ())), prefer...  13.8 us
  transfers between devices with their start and end apart: 6, of which 5 were waited for; matrix products, arithmetic and copies ran while one was open for 15% of the time, Pallas kernels for 0%

commit v1 on v0

--- a/solution.py
+++ b/solution.py
@@ -2,10 +2,25 @@
 import jax.numpy as jnp
 from jax import lax
 from jax.sharding import PartitionSpec as P
+from jax.lax import axis_index, axis_size, ppermute
 
 HD = 256
 BLK = 128
 masked_value = -1e30
+
+
+def write_array(x_part, a_name="dp"):
+    width = axis_size(a_name)
+    table = list(map(lambda at: (at, (at + 1) % width), range(width)))
+    items = list(map(lambda at: (at, (at - 1) % width), range(width)))
+    part_next, back = ([x_part], [x_part])
+    for _ in range(width // 2):
+        part_next.append(ppermute(part_next[-1], a_name, table))
+    for _ in range((width - 1) // 2):
+        back.append(ppermute(back[-1], a_name, items))
+    clean = jnp.concatenate([*part_next[::-1], *back[1:]], axis=0)
+    left_arr = jnp.roll(clean, (axis_index(a_name) - width // 2) * x_part.shape[0], axis=0)
+    return left_arr
 
 
 def attend_weights(scores, live_mask):
@@ -36,7 +51,7 @@
 ):
     bin_count = lax.axis_size("dp")
     full_key, full_value = (
-        lax.all_gather(key_weight, "dp", axis=0, tiled=True),
+        write_array(key_weight),
         lax.all_gather(value_weight, "dp", axis=0, tiled=True),
     )
     head_width = full_key.shape[1]

time: 428 us -> 419 us (0.979)
  waiting for transfers between devices: 268 us -> 254 us
  starting transfers between devices: 9.53 us -> 20.6 us
  local copies, waits for them, and re-layouts: 44.9 us -> 38.9 us
    ppermute x0 -> x7, waiting for transfers between devices: none -> 53.4 us  [the longest x4 47 us: write_array(): part_next.append(ppermute(part_next[-1], a_name, table))]
    all_gather x1, waiting for transfers between devices: 34 us -> 0.01 us  [per_device(): lax.all_gather(value_weight, 'dp', axis=0, tiled=True)]
    all_gather x1 -> x0, waiting for transfers between devices: 33.8 us -> none  [per_device(): lax.all_gather(key_weight, 'dp', axis=0, tiled=True)]
    ppermute x0 -> x7, starting transfers between devices: none -> 8.53 us  [the longest x3 7.97 us: write_array(): back.append(ppermute(back[-1], a_name, items))]
    concatenate x1, local copies, waits for them, and re-layouts: 4.46 us -> 0.04 us  [write_array(): jnp.roll(clean, (axis_index(a_name) - width // 2) * x_part.shape[0], axis=0)]
    unnamed x24 -> x40, local copies, waits for them, and re-layouts: 15.9 us -> 12 us
  transfers between devices with their start and end apart: 6 -> 12, of which waited for: 5 -> 7; matrix products, arithmetic and copies ran while one was open for 15% -> 13% of each run, Pallas kernels for 0% -> 0%
where the time goes in v1:
time: 419 us
  waiting for transfers between devices  254 us (61%)
  matrix products  60.9 us (15%)
  local copies, waits for them, and re-layouts  38.9 us (9%)
  blocking collectives  29 us (7%)
  starting transfers between devices  20.6 us (5%)
  between operations  14.1 us (3%)
    reduce_scatter x1, waiting for transfers between devices, per_device(): lax.psum_scatter(row_terms.astype(jnp.bfloat16), 'mp', scatter_dimension=...  127 us
    ppermute x4, waiting for transfers between devices, write_array(): part_next.append(ppermute(part_next[-1], a_name, table))  47 us
    reduce_scatter x1, waiting for transfers between devices, per_device(): lax.psum_scatter(weight_terms.astype(jnp.bfloat16), 'dp', scatter_dimensi...  46.5 us
    all_to_all x1, blocking collectives, per_device(): lax.all_to_all(slot_grads, 'dp', split_axis=0, concat_axis=0, tiled=True)  29 us
    all_to_all x1, waiting for transfers between devices, per_device(): lax.all_to_all(outbound, 'dp', split_axis=0, concat_axis=0, tiled=True)  25.8 us
    dot_general x1, matrix products, per_device(): lax.dot_general(encoder_rows, own_grads, (((0,), (0,)), ((), ())), prefer...  13.9 us
    dot_general x1, matrix products, per_device(): lax.dot_general(own_grads, both_weights, (((1,), (1,)), ((), ())), prefer...  13.5 us
    dot_general x1, matrix products, per_device(): jnp.dot(encoder_rows, both_weights, preferred_element_type=jnp.float32)  13.5 us
  transfers between devices with their start and end apart: 12, of which 7 were waited for; matrix products, arithmetic and copies ran while one was open for 13% of the time, Pallas kernels for 0%

profile of v1, /device:TPU:0, one launch (start us, length us, event | category | flops | bytes accessed | tf_op | source)
XLA Modules:
  0.0 418.6 jit_solution(10139530978027451725)
XLA Ops:
  8.4 9.9 %collective-permute-done = bf16[512,512]{1,0:T(8,128)(2,1)S(1)} collective-permute-done((bf16[512,512]{1,0:T(8,128)(2,1)}, bf16[512,512]{1,0:T(8,128)(2,1)S(1)}, u32[]{:S(2)}, u32[]{:S(2)}) %collective-permute-start) | collective-permute-done | bytes 524320 | tf_op jit(solution)/shard_map/ppermute | solution.py:18
  18.4 2.6 collective-permute-start.4
  21.0 16.5 %collective-permute-done.1 = bf16[512,512]{1,0:T(8,128)(2,1)S(1)} collective-permute-done((bf16[512,512]{1,0:T(8,128)(2,1)S(1)}, bf16[512,512]{1,0:T(8,128)(2,1)S(1)}, u32[]{:S(2)}, u32[]{:S(2)}) %collective-permute-start.1) | collective-permute-done | bytes 524320 | tf_op jit(solution)/shard_map/ppermute | solution.py:18
  37.6 2.6 collective-permute-start.5
  40.2 20.5 %collective-permute-done.2 = bf16[512,512]{1,0:T(8,128)(2,1)S(1)} collective-permute-done((bf16[512,512]{1,0:T(8,128)(2,1)S(1)}, bf16[512,512]{1,0:T(8,128)(2,1)S(1)}, u32[]{:S(2)}, u32[]{:S(2)}) %collective-permute-start.2) | collective-permute-done | bytes 524320 | tf_op jit(solution)/shard_map/ppermute | solution.py:18
  62.3 7.3 %all-to-all-start.1 = ((bf16[8,1,128]{2,1,0:T(2,128)(2,1)}), bf16[8,1,128]{2,1,0:T(2,128)(2,1)S(1)}, u32[]{:S(2)}, u32[]{:S(2)}) async-start(bf16[8,1,128]{2,1,0:T(2,128)(2,1)} %broadcast_in_dim.30), calls=%async_computation.1 | async-start | bytes 8192 | tf_op jit(solution)/shard_map/all_to_all | solution.py:84
  69.6 2.7 collective-permute-start.6
  72.7 6.4 %collective-permute-done.6 = bf16[512,512]{1,0:T(8,128)(2,1)S(1)} collective-permute-done((bf16[512,512]{1,0:T(8,128)(2,1)S(1)}, bf16[512,512]{1,0:T(8,128)(2,1)S(1)}, u32[]{:S(2)}, u32[]{:S(2)}) %collective-permute-start.6) | collective-permute-done | bytes 524320 | tf_op jit(solution)/shard_map/ppermute | solution.py:20
  81.7 13.5 %convert_bitcast_fusion.1 = bf16[896,1024]{0,1:T(8,128)(2,1)S(1)} fusion(bf16[896,4096]{1,0:T(8,128)(2,1)} %param.10, bf16[4096,512]{1,0:T(8,128)(2,1)} %all-gather.2.cloned.1.call-done, bf16[4096,512]{1,0:T(8,128)(2,1)} %constant_dynamic-slice_fusion), kind=kOutput, calls=%fused_computation.18 | convolution fusion | flops 7533887488 | bytes 17563648 | tf_op jit(solution)/shard_map/dot_general | solution.py:62
  95.2 2.4 copy.79
  97.6 3.8 reshape.137
  103.6 4.1 copy.80
  107.8 4.2 %all-to-all-start = ((bf16[8,128,1024]{1,2,0:T(8,128)(2,1)}), bf16[8,128,1024]{1,2,0:T(8,128)(2,1)S(1)}, u32[]{:S(2)}, u32[]{:S(2)}) async-start(bf16[8,128,1024]{1,2,0:T(8,128)(2,1)} %copy.80), calls=%async_computation | async-start | bytes 4194304 | tf_op jit(solution)/shard_map/all_to_all | solution.py:83
  112.7 25.8 %all-to-all-done = bf16[8,128,1024]{1,2,0:T(8,128)(2,1)S(1)} async-done(((bf16[8,128,1024]{1,2,0:T(8,128)(2,1)}), bf16[8,128,1024]{1,2,0:T(8,128)(2,1)S(1)}, u32[]{:S(2)}, u32[]{:S(2)}) %all-to-all-start) | async-done | bytes 2097184 | tf_op jit(solution)/shard_map/all_to_all | solution.py:83
  148.5 6.2 %fusion.10 = bf16[1024,2,256]{2,0,1:T(8,128)(2,1)} fusion(f32[2,1024,256]{2,1,0:T(8,128)} %fusion.18, bf16[32,2,8,256]{3,2,1,0:T(8,128)(2,1)} %bitcast.134, f32[2,1024,256]{2,1,0:T(8,128)} %copy-done.1, f32[2,256]{1,0:T(2,128)S(1)} %broadcast_maximum_fusion, f32[2,256]{1,0:T(2,128)S(1)} %broadcast_select_fusion, pred[256,1024]{0,1:T(8,128)(4,1)S(1)} %get-tuple-element.35), kind=kOutput, calls=%fused_computation.23 | convolution fusion | flops 275777024 | bytes 5771264 | tf_op jit(solution)/shard_map/hts,thd->shd/dot_general | solution.py:111
  156.9 29.0 %all_to_all.16 = bf16[8,128,1024]{1,2,0:T(8,128)(2,1)S(1)} all-to-all(bf16[8,128,1024]{1,2,0:T(8,128)(2,1)S(1)} %copy.93), channel_id=1, replica_groups=mesh['dp'=8,'mp'=4] {'dp'}, dimensions={0} | all-to-all | bytes 4194304 | tf_op jit(solution)/shard_map/all_to_all | solution.py:124
  185.9 2.6 copy.94
  188.5 2.7 copy.107
  192.0 4.0 reshape.150
  196.0 13.9 %convert_bitcast_fusion = bf16[4096,1024]{0,1:T(8,128)(2,1)} fusion(bf16[896,1024]{1,0:T(8,128)(2,1)} %reshape.150, bf16[896,4096]{1,0:T(8,128)(2,1)} %param.10), kind=kOutput, calls=%fused_computation.4 | convolution fusion | flops 7520387072 | bytes 17563648 | tf_op jit(solution)/shard_map/dot_general | solution.py:131
  211.4 13.5 %convolution_convert_fusion.2 = bf16[896,4096]{1,0:T(8,128)(2,1)} fusion(bf16[896,1024]{1,0:T(8,128)(2,1)S(1)} %copy-done.4, bf16[4096,512]{1,0:T(8,128)(2,1)} %all-gather.2.cloned.1.call-done, bf16[4096,512]{1,0:T(8,128)(2,1)} %constant_dynamic-slice_fusion), kind=kOutput, calls=%fused_computation.5 | convolution fusion | flops 7536640000 | bytes 17563648 | tf_op jit(solution)/shard_map/dot_general | solution.py:139
  229.8 4.2 %convolution_convert_fusion.5 = bf16[2,256,256]{2,1,0:T(8,128)(2,1)S(1)} fusion(bf16[1024,2,256]{0,2,1:T(8,128)(2,1)} %copy-done.5, f32[2,1024,256]{2,1,0:T(8,128)} %fusion.18, f32[2,1024,256]{2,1,0:T(8,128)S(1)} %copy-done.2, f32[2,256]{1,0:T(2,128)S(1)} %broadcast_maximum_fusion, f32[2,256]{1,0:T(2,128)S(1)} %broadcast_select_fusion, ...), kind=kOutput, calls=%fused_computation.25 | convolution fusion | flops 275383808 | bytes 5771264 | tf_op jit(solution)/shard_map/hts,shd->thd/dot_general | solution.py:108
  234.9 46.5 %reduce-scatter.5.cloned.1.call-done = bf16[512,1024]{0,1:T(8,128)(2,1)} async-done(((bf16[4096,1024]{0,1:T(8,128)(2,1)}), bf16[512,1024]{0,1:T(8,128)(2,1)}) %reduce-scatter.5.cloned.1.call-update) | async-done | bytes 1048592 | tf_op jit(solution)/shard_map/reduce_scatter | solution.py:134
  284.6 127.4 %reduce-scatter.3.cloned.1.call-done = bf16[896,1024]{1,0:T(8,128)(2,1)} async-done(((bf16[896,4096]{1,0:T(8,128)(2,1)}), bf16[896,1024]{1,0:T(8,128)(2,1)}) %reduce-scatter.3.cloned.1.call-update) | async-done | bytes 1835024 | tf_op jit(solution)/shard_map/reduce_scatter | solution.py:142
  (82 shorter events, 32.0 us)
Async XLA Ops:
  7.2 74.5 %all-gather.2.cloned.1.call-start = ((), (), s32[]{:S(2)}) async-start(), calls=%async_computation.5 | async-start | bytes 4718592 | tf_op jit(solution)/shard_map/all_gather | solution.py:55
  7.9 10.5 %collective-permute-start = (bf16[512,512]{1,0:T(8,128)(2,1)}, bf16[512,512]{1,0:T(8,128)(2,1)S(1)}, u32[]{:S(2)}, u32[]{:S(2)}) collective-permute-start(bf16[512,512]{1,0:T(8,128)(2,1)} %param.11), channel_id=1, source_target_pairs={{0,4},{4,8},{8,12},{12,16},{16,20},{20,24},{24,28},{28,0},{1,5},{5... | collective-permute-start | bytes 1572872 | tf_op jit(solution)/shard_map/ppermute | solution.py:18
  18.4 19.2 %collective-permute-start.1 = (bf16[512,512]{1,0:T(8,128)(2,1)S(1)}, bf16[512,512]{1,0:T(8,128)(2,1)S(1)}, u32[]{:S(2)}, u32[]{:S(2)}) collective-permute-start(bf16[512,512]{1,0:T(8,128)(2,1)S(1)} %collective-permute-done), channel_id=1, source_target_pairs={{0,4},{4,8},{8,12},{12,16},{16,20},{20,24},{24,28},{28,0},{1,5},{5... | collective-permute-start | bytes 1572872 | tf_op jit(solution)/shard_map/ppermute | solution.py:18
  18.4 19.2 %collective-permute-start.4 = (bf16[512,512]{1,0:T(8,128)(2,1)}, bf16[512,512]{1,0:T(8,128)(2,1)S(1)}, u32[]{:S(2)}, u32[]{:S(2)}) collective-permute-start(bf16[512,512]{1,0:T(8,128)(2,1)} %param.11), channel_id=1, source_target_pairs={{0,28},{4,0},{8,4},{12,8},{16,12},{20,16},{24,20},{28,24},{1,29},{... | collective-permute-start | bytes 1572872 | tf_op jit(solution)/shard_map/ppermute | solution.py:20
  37.6 23.2 %collective-permute-start.2 = (bf16[512,512]{1,0:T(8,128)(2,1)S(1)}, bf16[512,512]{1,0:T(8,128)(2,1)S(1)}, u32[]{:S(2)}, u32[]{:S(2)}) collective-permute-start(bf16[512,512]{1,0:T(8,128)(2,1)S(1)} %collective-permute-done.1), channel_id=1, source_target_pairs={{0,4},{4,8},{8,12},{12,16},{16,20},{20,24},{24,28},{28,0},{1,5},{5... | collective-permute-start | bytes 1572872 | tf_op jit(solution)/shard_map/ppermute | solution.py:18
  37.6 32.1 %collective-permute-start.5 = (bf16[512,512]{1,0:T(8,128)(2,1)S(1)}, bf16[512,512]{1,0:T(8,128)(2,1)S(1)}, u32[]{:S(2)}, u32[]{:S(2)}) collective-permute-start(bf16[512,512]{1,0:T(8,128)(2,1)S(1)} %collective-permute-done.4), channel_id=1, source_target_pairs={{0,28},{4,0},{8,4},{12,8},{16,12},{20,16},{24,20},{28,24},{1,29},{... | collective-permute-start | bytes 1572872 | tf_op jit(solution)/shard_map/ppermute | solution.py:20
  60.8 11.6 %collective-permute-start.3 = (bf16[512,512]{1,0:T(8,128)(2,1)S(1)}, bf16[512,512]{1,0:T(8,128)(2,1)S(1)}, u32[]{:S(2)}, u32[]{:S(2)}) collective-permute-start(bf16[512,512]{1,0:T(8,128)(2,1)S(1)} %collective-permute-done.2), channel_id=1, source_target_pairs={{0,4},{4,8},{8,12},{12,16},{16,20},{20,24},{24,28},{28,0},{1,5},{5... | collective-permute-start | bytes 1572872 | tf_op jit(solution)/shard_map/ppermute | solution.py:18
  62.3 45.4 %all-to-all-start.1 = ((bf16[8,1,128]{2,1,0:T(2,128)(2,1)}), bf16[8,1,128]{2,1,0:T(2,128)(2,1)S(1)}, u32[]{:S(2)}, u32[]{:S(2)}) async-start(bf16[8,1,128]{2,1,0:T(2,128)(2,1)} %broadcast_in_dim.30), calls=%async_computation.1 | async-start | bytes 8192 | tf_op jit(solution)/shard_map/all_to_all | solution.py:84
  69.6 2.9 copy-start.3
  69.6 9.4 %collective-permute-start.6 = (bf16[512,512]{1,0:T(8,128)(2,1)S(1)}, bf16[512,512]{1,0:T(8,128)(2,1)S(1)}, u32[]{:S(2)}, u32[]{:S(2)}) collective-permute-start(bf16[512,512]{1,0:T(8,128)(2,1)S(1)} %collective-permute-done.5), channel_id=1, source_target_pairs={{0,28},{4,0},{8,4},{12,8},{16,12},{20,16},{24,20},{28,24},{1,29},{... | collective-permute-start | bytes 1572872 | tf_op jit(solution)/shard_map/ppermute | solution.py:20
  97.6 3.8 copy-start.7
  107.7 4.5 %copy-start.8 = (s32[1,4]{1,0:T(1,128)S(1)}, s32[1,4]{1,0:T(1,128)}, u32[]{:S(2)}) copy-start(s32[1,4]{1,0:T(1,128)} %param.13) | copy-start | bytes 52
  107.8 30.8 %all-to-all-start = ((bf16[8,128,1024]{1,2,0:T(8,128)(2,1)}), bf16[8,128,1024]{1,2,0:T(8,128)(2,1)S(1)}, u32[]{:S(2)}, u32[]{:S(2)}) async-start(bf16[8,128,1024]{1,2,0:T(8,128)(2,1)} %copy.80), calls=%async_computation | async-start | bytes 4194304 | tf_op jit(solution)/shard_map/all_to_all | solution.py:83
  112.0 169.4 %reduce-scatter.5.cloned.1.call-start = ((), (), s32[]{:S(2)}) async-start(), calls=%async_computation.7 | async-start | bytes 9437184 | tf_op jit(solution)/shard_map/reduce_scatter | solution.py:134
  139.7 1.2 copy-start
  142.1 2.3 copy-start.5
  143.9 3.1 copy-start.1
  143.9 1.1 copy-start.6
  209.9 1.5 copy-start.4
  209.9 202.1 %reduce-scatter.3.cloned.1.call-start = ((), (), s32[]{:S(2)}) async-start(), calls=%async_computation.6 | async-start | bytes 9175040 | tf_op jit(solution)/shard_map/reduce_scatter | solution.py:142
  224.9 1.7 copy-start.2
Sparse Core Ops, SparseCore 0:
  9.9 55.0 all-gather.1
  210.0 71.2 reduce-scatter.4
  284.2 127.7 reduce-scatter.2
